TPU v7x, 512 devices: a whole 4x8x8 slice. The times are simulated.
512 devices in a mesh: vocab: 64 (over y, z_hi, core), width: 8 (over z_lo, x).
Axes of the slice: x: 4, y: 8, z: 8 (z_hi: 4, z_lo: 2; z = z_hi * 2 + z_lo), core: 2. Of those that a mesh axis runs over, the one named last changes fastest.
Arguments:
- head_weight: bfloat16 [4096, 65536], P('width', 'vocab'), may hold values from -3 to 3
- direction: bfloat16 [4096, 65536], P('width', 'vocab'), may hold values from -150 to 150
- residual: bfloat16 [4096, 65536], P('width', 'vocab'), may hold values from -150 to 150
- hidden: bfloat16 [512, 4096], P('vocab', 'width'), may hold values from -200 to 200
- fold_ids: int32 [512], replicated, may hold values from 0 to 7
Outputs:
- new_direction: bfloat16 [4096, 65536], P('width', 'vocab')
All inputs are finite; a program needn't handle non-finite values.
Results may differ from a plain program's by a relative error of at most 0.0085.
Values may be sent and summed in bfloat16 or wider, within the bound.
A program may use at most 64 MiB of HBM per device.

v0:
```python
import jax
import jax.numpy as jnp
from jax import lax
from jax.sharding import PartitionSpec as P

DAMPING = 0.02
CONTRACT_LEAD = (((0,), (1,)), ((), ()))


def local(head_weight, direction, residual, hidden, fold_ids):
    wide_panel = lax.all_gather(hidden, "width", axis=1, tiled=True)
    panels = lax.all_gather(wide_panel, "vocab", axis=0, tiled=True)
    weight_cols, direction_cols = (
        lax.all_to_all(head_weight, "width", split_axis=1, concat_axis=0, tiled=True),
        lax.all_to_all(direction, "width", split_axis=1, concat_axis=0, tiled=True),
    )
    logit_rows = lax.dot_general(
        weight_cols, panels, CONTRACT_LEAD, preferred_element_type=jnp.float32
    )
    tangent_rows = lax.dot_general(
        direction_cols, panels, CONTRACT_LEAD, preferred_element_type=jnp.float32
    )
    local_top = jnp.max(logit_rows, axis=0)
    row_top = lax.pmax(local_top, ("vocab", "width"))
    weights = jnp.exp(logit_rows - row_top[None, :])
    row_total, row_moment = lax.psum(
        (jnp.sum(weights, axis=0), jnp.sum(weights * tangent_rows, axis=0)), ("vocab", "width")
    )
    kept_mask = (fold_ids != 0).astype(jnp.float32)
    row_mean = row_moment / row_total
    curving = (
        kept_mask[None, :] * (weights / row_total[None, :]) * (tangent_rows - row_mean[None, :])
    ).astype(jnp.bfloat16)
    column_block = lax.dot_general(
        panels, curving, CONTRACT_LEAD, preferred_element_type=jnp.float32
    )
    curvature = lax.all_to_all(column_block, "width", split_axis=0, concat_axis=1, tiled=True)
    direction_wide = direction.astype(jnp.float32)
    residual_wide = residual.astype(jnp.float32)
    operator_image = curvature + DAMPING * direction_wide
    squares, curvature_sum = lax.psum(
        (jnp.sum(residual_wide * residual_wide), jnp.sum(direction_wide * operator_image)),
        ("vocab", "width"),
    )
    step_size = squares / curvature_sum
    moved = residual_wide - step_size * operator_image
    next_squares = lax.psum(jnp.sum(moved * moved), ("vocab", "width"))
    mixing = next_squares / squares
    return (moved + mixing * direction_wide).astype(jnp.bfloat16)


def solution(mesh):
    placed = (
        P("width", "vocab"),
        P("width", "vocab"),
        P("width", "vocab"),
        P("vocab", "width"),
        P(),
    )
    return jax.shard_map(
        local, mesh=mesh, in_specs=placed, out_specs=P("width", "vocab"), check_vma=False
    )
```

profile of v0, /device:TPU:1, one launch (start us, length us, event | category | flops | bytes accessed | tf_op | source)
XLA Modules:
  0.0 570.6 jit_solution(6129876579250119001)
XLA Ops:
  6.5 0.0 all-gather.2.cloned.1.call-start
  6.5 26.3 %all_gather.6 = bf16[8,4096]{1,0:T(8,128)(2,1)} all-gather(bf16[8,512]{1,0:T(8,128)(2,1)} %param.8), channel_id=1, replica_groups=mesh['vocab'=64,'width'=8] {'width'}, dimensions={1}, use_global_device_ids=true | all-gather | bytes 73728 | tf_op jit(solution)/shard_map/all_gather | solution.py:11
  32.8 0.0 all-gather.2.cloned.1.call-update
  32.8 0.0 copy-start
  32.9 2.4 copy.13
  35.2 4.1 all-to-all-start
  39.3 0.0 copy-done
  39.3 0.0 copy-start.1
  39.4 1.3 copy.15
  40.7 8.1 %all-to-all-done = bf16[512,8,128]{0,2,1:T(8,128)(2,1)S(1)} async-done(((bf16[512,8,128]{0,2,1:T(8,128)(2,1)}), bf16[512,8,128]{0,2,1:T(8,128)(2,1)S(1)}, u32[]{:S(2)}, u32[]{:S(2)}) %all-to-all-start) | async-done | bytes 1048608 | tf_op jit(solution)/shard_map/all_to_all | solution.py:14
  48.8 4.2 all-to-all-start.1
  53.0 0.0 copy-done.1
  53.1 0.7 copy.14
  53.7 11.8 %all-to-all-done.1 = bf16[512,8,128]{0,2,1:T(8,128)(2,1)} async-done(((bf16[512,8,128]{0,2,1:T(8,128)(2,1)}), bf16[512,8,128]{0,2,1:T(8,128)(2,1)}, u32[]{:S(2)}, u32[]{:S(2)}) %all-to-all-start.1) | async-done | bytes 1048608 | tf_op jit(solution)/shard_map/all_to_all | solution.py:15
  65.5 1.6 copy.16
  67.2 64.0 %all-gather.2.cloned.1.call-done = bf16[512,4096]{1,0:T(8,128)(2,1)} async-done(((bf16[8,4096]{1,0:T(8,128)(2,1)}), bf16[512,4096]{1,0:T(8,128)(2,1)}) %all-gather.2.cloned.1.call-update) | async-done | bytes 4194320 | tf_op jit(solution)/shard_map/all_gather | solution.py:12
  131.1 3.7 fusion.11
  134.8 96.2 %pmax.7 = f32[512]{0:T(512)S(1)} all-reduce(f32[512]{0:T(512)S(1)} %get-tuple-element.11), channel_id=1, replica_groups=mesh['vocab'=64,'width'=8] {'vocab','width'}, use_global_device_ids=true, to_apply=%region_3.0 | all-reduce | flops 512 | bytes 4096 | tf_op jit(solution)/shard_map/pmax | solution.py:24
  231.0 3.7 fusion.5
  234.7 93.4 %all-reduce.1 = (f32[512]{0:T(512)S(1)}, f32[512]{0:T(512)S(1)}) all-reduce(f32[512]{0:T(512)S(1)} %get-tuple-element.6, f32[512]{0:T(512)S(1)} %get-tuple-element.5), channel_id=1, replica_groups=mesh['vocab'=64,'width'=8] {'vocab','width'}, use_global_device_ids=true, to_apply=%region_7.0 | all-reduce | flops 1024 | bytes 8192 | tf_op jit(solution)/shard_map/psum | solution.py:26
  328.1 2.9 fusion.6
  331.1 0.2 copy.21
  331.3 29.6 %all_to_all.57 = f32[8,512,128]{1,2,0:T(8,128)} all-to-all(f32[8,512,128]{1,2,0:T(8,128)S(1)} %bitcast.19), channel_id=1, replica_groups=mesh['vocab'=64,'width'=8] {'width'}, dimensions={0} | all-to-all | bytes 4194304 | tf_op jit(solution)/shard_map/all_to_all | solution.py:37
  360.9 1.9 copy.18
  362.8 2.5 fusion
  365.3 95.9 %all-reduce = (f32[]{:T(128)}, f32[]{:T(128)}) all-reduce(f32[]{:T(128)} %get-tuple-element.14, f32[]{:T(128)} %get-tuple-element.15), channel_id=1, replica_groups=mesh['vocab'=64,'width'=8] {'vocab','width'}, use_global_device_ids=true, to_apply=%region_1.0 | all-reduce | flops 2 | bytes 16 | tf_op jit(solution)/shard_map/psum | solution.py:41
  462.4 2.5 multiply_reduce_fusion
  464.9 94.6 %psum.39 = f32[]{:T(128)} all-reduce(f32[]{:T(128)} %multiply_reduce_fusion), channel_id=1, replica_groups=mesh['vocab'=64,'width'=8] {'vocab','width'}, use_global_device_ids=true, to_apply=%region_11.0 | all-reduce | flops 1 | bytes 8 | tf_op jit(solution)/shard_map/psum | solution.py:47
  560.9 2.8 fusion.4
  (2 shorter events, 0.0 us)
Async XLA Ops:
  6.5 124.6 %all-gather.2.cloned.1.call-start = ((), (), s32[]{:S(2)}) async-start(), calls=%async_computation.3 | async-start | bytes 4259840 | tf_op jit(solution)/shard_map/all_gather | solution.py:12
  32.8 6.5 %copy-start = (bf16[512,1024]{1,0:T(8,128)(2,1)S(1)}, bf16[512,1024]{1,0:T(8,128)(2,1)}, u32[]{:S(2)}) copy-start(bf16[512,1024]{1,0:T(8,128)(2,1)} %param.6) | copy-start | bytes 3145732
  35.2 13.6 %all-to-all-start = ((bf16[512,8,128]{0,2,1:T(8,128)(2,1)}), bf16[512,8,128]{0,2,1:T(8,128)(2,1)S(1)}, u32[]{:S(2)}, u32[]{:S(2)}) async-start(bf16[512,8,128]{0,2,1:T(8,128)(2,1)} %bitcast), calls=%async_computation | async-start | bytes 2097152 | tf_op jit(solution)/shard_map/all_to_all | solution.py:14
  39.3 13.7 %copy-start.1 = (s32[512]{0:T(512)S(1)}, s32[512]{0:T(512)}, u32[]{:S(2)}) copy-start(s32[512]{0:T(512)} %param.9) | copy-start | bytes 6148
  48.8 16.8 %all-to-all-start.1 = ((bf16[512,8,128]{0,2,1:T(8,128)(2,1)}), bf16[512,8,128]{0,2,1:T(8,128)(2,1)}, u32[]{:S(2)}, u32[]{:S(2)}) async-start(bf16[512,8,128]{0,2,1:T(8,128)(2,1)} %bitcast.3), calls=%async_computation.1 | async-start | bytes 2097152 | tf_op jit(solution)/shard_map/all_to_all | solution.py:15
Sparse Core Ops, SparseCore 0:
  33.0 98.1 all-gather.1
where the time goes:
time: 571 us
  blocking collectives  436 us (76%)
  waiting for transfers between devices  83.9 us (15%)
  between operations  16.1 us (3%)
  matrix products  10.4 us (2%)
  starting transfers between devices  8.36 us (1%)
  local copies, waits for them, and re-layouts  8.15 us (1%)
  other arithmetic  7.74 us (1%)
    pmax x1, blocking collectives, local(): row_top = lax.pmax(local_top, ('vocab', 'width'))  96.2 us
    psum x1, blocking collectives, local(): lax.psum((jnp.sum(residual_wide * residual_wide), jnp.sum(direction_wide...  95.9 us
    psum x1, blocking collectives, local(): next_squares = lax.psum(jnp.sum(moved * moved), ('vocab', 'width'))  94.6 us
    psum x1, blocking collectives, local(): lax.psum((jnp.sum(weights, axis=0), jnp.sum(weights * tangent_rows, axis=...  93.4 us
    all_gather x1, waiting for transfers between devices, local(): panels = lax.all_gather(wide_panel, 'vocab', axis=0, tiled=True)  64 us
    all_to_all x1, blocking collectives, local(): lax.all_to_all(column_block, 'width', split_axis=0, concat_axis=1, tiled=...  29.6 us
    all_gather x1, blocking collectives, local(): wide_panel = lax.all_gather(hidden, 'width', axis=1, tiled=True)  26.3 us
    all_to_all x1, waiting for transfers between devices, local(): lax.all_to_all(direction, 'width', split_axis=1, concat_axis=0, tiled=True)  11.8 us
  transfers between devices with their start and end apart: 3, of which 3 were waited for; matrix products, arithmetic and copies ran while one was open for 1% of the time, Pallas kernels for 0%

commit v1 on v0

--- a/solution.py
+++ b/solution.py
@@ -8,7 +8,9 @@
 
 
 def local(head_weight, direction, residual, hidden, fold_ids):
-    wide_panel = lax.all_gather(hidden, "width", axis=1, tiled=True)
+    wide_panel = jnp.concatenate(
+        lax.all_to_all(jnp.stack([hidden] * lax.axis_size("width")), "width", 0, 0), axis=1
+    )
     panels = lax.all_gather(wide_panel, "vocab", axis=0, tiled=True)
     weight_cols, direction_cols = (
         lax.all_to_all(head_weight, "width", split_axis=1, concat_axis=0, tiled=True),

time: 571 us -> 552 us (0.967)
  blocking collectives: 436 us -> 421 us
  waiting for transfers between devices: 83.9 us -> 75.2 us
    all_gather x1 -> x0, blocking collectives: 26.3 us -> none  [local(): wide_panel = lax.all_gather(hidden, 'width', axis=1, tiled=True)]
    all_to_all x0 -> x1, blocking collectives: none -> 11.7 us  [local(): lax.all_to_all(jnp.stack([hidden] * lax.axis_size('width')), 'width', 0, 0)]
    all_gather x1, waiting for transfers between devices: 64 us -> 52.4 us  [local(): panels = lax.all_gather(wide_panel, 'vocab', axis=0, tiled=True)]
where the time goes in v1:
time: 552 us; the launch traced here: 551 us
  blocking collectives  421 us (76%)
  waiting for transfers between devices  75.2 us (14%)
  between operations  16.1 us (3%)
  starting transfers between devices  11 us (2%)
  matrix products  10.4 us (2%)
  local copies, waits for them, and re-layouts  8.85 us (2%)
  other arithmetic  7.74 us (1%)
    pmax x1, blocking collectives, local(): row_top = lax.pmax(local_top, ('vocab', 'width'))  96.2 us
    psum x1, blocking collectives, local(): lax.psum((jnp.sum(residual_wide * residual_wide), jnp.sum(direction_wide...  95.9 us
    psum x1, blocking collectives, local(): next_squares = lax.psum(jnp.sum(moved * moved), ('vocab', 'width'))  94.7 us
    psum x1, blocking collectives, local(): lax.psum((jnp.sum(weights, axis=0), jnp.sum(weights * tangent_rows, axis=...  93.4 us
    all_gather x1, waiting for transfers between devices, local(): panels = lax.all_gather(wide_panel, 'vocab', axis=0, tiled=True)  52.4 us
    all_to_all x1, blocking collectives, local(): lax.all_to_all(column_block, 'width', split_axis=0, concat_axis=1, tiled=...  29.6 us
    all_to_all x1, waiting for transfers between devices, local(): lax.all_to_all(direction, 'width', split_axis=1, concat_axis=0, tiled=True)  14.4 us
    all_to_all x1, blocking collectives, local(): lax.all_to_all(jnp.stack([hidden] * lax.axis_size('width')), 'width', 0, 0)  11.7 us
  transfers between devices with their start and end apart: 3, of which 3 were waited for; matrix products, arithmetic and copies ran while one was open for 1% of the time, Pallas kernels for 0%

profile of v1, /device:TPU:1, one launch (start us, length us, event | category | flops | bytes accessed | tf_op | source)
XLA Modules:
  0.0 550.8 jit_solution(3807200322579672560)
XLA Ops:
  6.5 0.0 all-gather.2.cloned.1.call-start
  6.5 0.7 stack.2
  7.2 11.7 %all_to_all.62 = bf16[8,8,512]{2,1,0:T(8,128)(2,1)} all-to-all(bf16[8,8,512]{2,1,0:T(8,128)(2,1)S(1)} %stack.2), channel_id=1, replica_groups=mesh['vocab'=64,'width'=8] {'width'}, dimensions={0} | all-to-all | bytes 131072 | tf_op jit(solution)/shard_map/all_to_all | solution.py:12
  19.0 0.0 all-gather.2.cloned.1.call-update
  19.0 0.0 copy-start
  19.0 2.4 copy.13
  21.4 3.6 all-to-all-start
  24.9 0.0 copy-done
  25.0 0.0 copy-start.1
  25.0 1.3 copy.15
  26.3 8.4 %all-to-all-done = bf16[512,8,128]{0,2,1:T(8,128)(2,1)S(1)} async-done(((bf16[512,8,128]{0,2,1:T(8,128)(2,1)}), bf16[512,8,128]{0,2,1:T(8,128)(2,1)S(1)}, u32[]{:S(2)}, u32[]{:S(2)}) %all-to-all-start) | async-done | bytes 1048608 | tf_op jit(solution)/shard_map/all_to_all | solution.py:16
  34.7 7.5 %all-to-all-start.2 = ((bf16[512,8,128]{0,2,1:T(8,128)(2,1)}), bf16[512,8,128]{0,2,1:T(8,128)(2,1)}, u32[]{:S(2)}, u32[]{:S(2)}) async-start(bf16[512,8,128]{0,2,1:T(8,128)(2,1)} %bitcast.5), calls=%async_computation.2 | async-start | bytes 2097152 | tf_op jit(solution)/shard_map/all_to_all | solution.py:17
  42.2 0.0 copy-done.1
  42.2 0.7 copy.14
  42.9 14.4 %all-to-all-done.2 = bf16[512,8,128]{0,2,1:T(8,128)(2,1)} async-done(((bf16[512,8,128]{0,2,1:T(8,128)(2,1)}), bf16[512,8,128]{0,2,1:T(8,128)(2,1)}, u32[]{:S(2)}, u32[]{:S(2)}) %all-to-all-start.2) | async-done | bytes 1048608 | tf_op jit(solution)/shard_map/all_to_all | solution.py:17
  57.3 1.6 copy.16
  58.9 52.4 %all-gather.2.cloned.1.call-done = bf16[512,4096]{1,0:T(8,128)(2,1)} async-done(((bf16[8,4096]{1,0:T(8,128)(2,1)}), bf16[512,4096]{1,0:T(8,128)(2,1)}) %all-gather.2.cloned.1.call-update) | async-done | bytes 4194320 | tf_op jit(solution)/shard_map/all_gather | solution.py:14
  111.3 3.7 fusion.11
  115.0 96.2 %pmax.7 = f32[512]{0:T(512)S(1)} all-reduce(f32[512]{0:T(512)S(1)} %get-tuple-element.11), channel_id=1, replica_groups=mesh['vocab'=64,'width'=8] {'vocab','width'}, use_global_device_ids=true, to_apply=%region_3.0 | all-reduce | flops 512 | bytes 4096 | tf_op jit(solution)/shard_map/pmax | solution.py:26
  211.2 3.7 fusion.5
  214.9 93.4 %all-reduce.1 = (f32[512]{0:T(512)S(1)}, f32[512]{0:T(512)S(1)}) all-reduce(f32[512]{0:T(512)S(1)} %get-tuple-element.6, f32[512]{0:T(512)S(1)} %get-tuple-element.5), channel_id=1, replica_groups=mesh['vocab'=64,'width'=8] {'vocab','width'}, use_global_device_ids=true, to_apply=%region_7.0 | all-reduce | flops 1024 | bytes 8192 | tf_op jit(solution)/shard_map/psum | solution.py:28
  308.3 2.9 fusion.6
  311.3 0.2 copy.21
  311.5 29.6 %all_to_all.63 = f32[8,512,128]{1,2,0:T(8,128)} all-to-all(f32[8,512,128]{1,2,0:T(8,128)S(1)} %bitcast.22), channel_id=1, replica_groups=mesh['vocab'=64,'width'=8] {'width'}, dimensions={0} | all-to-all | bytes 4194304 | tf_op jit(solution)/shard_map/all_to_all | solution.py:39
  341.1 1.9 copy.18
  343.0 2.5 fusion
  345.5 95.9 %all-reduce = (f32[]{:T(128)}, f32[]{:T(128)}) all-reduce(f32[]{:T(128)} %get-tuple-element.14, f32[]{:T(128)} %get-tuple-element.15), channel_id=1, replica_groups=mesh['vocab'=64,'width'=8] {'vocab','width'}, use_global_device_ids=true, to_apply=%region_1.0 | all-reduce | flops 2 | bytes 16 | tf_op jit(solution)/shard_map/psum | solution.py:43
  442.6 2.5 multiply_reduce_fusion
  445.1 94.7 %psum.39 = f32[]{:T(128)} all-reduce(f32[]{:T(128)} %multiply_reduce_fusion), channel_id=1, replica_groups=mesh['vocab'=64,'width'=8] {'vocab','width'}, use_global_device_ids=true, to_apply=%region_11.0 | all-reduce | flops 1 | bytes 8 | tf_op jit(solution)/shard_map/psum | solution.py:49
  541.1 2.8 fusion.4
  (2 shorter events, 0.0 us)
Async XLA Ops:
  6.5 104.8 %all-gather.2.cloned.1.call-start = ((), (), s32[]{:S(2)}) async-start(), calls=%async_computation.4 | async-start | bytes 4259840 | tf_op jit(solution)/shard_map/all_gather | solution.py:14
  19.0 5.9 %copy-start = (bf16[512,1024]{1,0:T(8,128)(2,1)S(1)}, bf16[512,1024]{1,0:T(8,128)(2,1)}, u32[]{:S(2)}) copy-start(bf16[512,1024]{1,0:T(8,128)(2,1)} %param.6) | copy-start | bytes 3145732
  21.4 13.4 %all-to-all-start = ((bf16[512,8,128]{0,2,1:T(8,128)(2,1)}), bf16[512,8,128]{0,2,1:T(8,128)(2,1)S(1)}, u32[]{:S(2)}, u32[]{:S(2)}) async-start(bf16[512,8,128]{0,2,1:T(8,128)(2,1)} %bitcast), calls=%async_computation | async-start | bytes 2097152 | tf_op jit(solution)/shard_map/all_to_all | solution.py:16
  25.0 17.3 %copy-start.1 = (s32[512]{0:T(512)S(1)}, s32[512]{0:T(512)}, u32[]{:S(2)}) copy-start(s32[512]{0:T(512)} %param.9) | copy-start | bytes 6148
  34.7 22.6 %all-to-all-start.2 = ((bf16[512,8,128]{0,2,1:T(8,128)(2,1)}), bf16[512,8,128]{0,2,1:T(8,128)(2,1)}, u32[]{:S(2)}, u32[]{:S(2)}) async-start(bf16[512,8,128]{0,2,1:T(8,128)(2,1)} %bitcast.5), calls=%async_computation.2 | async-start | bytes 2097152 | tf_op jit(solution)/shard_map/all_to_all | solution.py:17
Sparse Core Ops, SparseCore 0:
  19.1 92.1 all-gather.1
